TPU v7x, 512 devices: a whole 4x4x16 slice. The times are simulated.
512 devices in a mesh: term: 16 (over z), doc: 32 (over x, y, core).
Axes of the slice: x: 4, y: 4, z: 16, core: 2. Of those that a mesh axis runs over, the one named last changes fastest.
Arguments:
- postings: bfloat16 [16384, 30720], P('doc', 'term'), may hold values from 0 to 3
- query_terms: int32 [128, 32], replicated, may hold values from 0 to 30719
- query_levels: int32 [128, 32], replicated, may hold values from 1 to 255
- feedback_ids: int32 [128, 10], replicated, may hold values from 0 to 16383, as said below
Outputs:
- first_scores: float32 [128, 16384], P('term', 'doc')
- final_scores: float32 [128, 16384], P('term', 'doc')
Inputs may be any that keep to these rules, and one draw needn't show every extreme that they name: `feedback_ids`: the 1280 feedback ids are all different.
All inputs are finite; a program needn't handle non-finite values.
Results may differ from a plain program's by a relative error of at most 0.0015.
Values may be sent and summed in bfloat16 or wider, within the bound.
No kernel may reach another device: no remote copies, remote signals or barrier semaphores. Data moves between devices by JAX's collectives and lax.ppermute only.
A program may use at most 64 MiB of HBM per device.

v0:
```python
import jax
import jax.numpy as jnp
from jax import lax
from jax.sharding import PartitionSpec as P

expansion_weight = 0.25


def query_slice(query_terms, query_levels, width, offset):
    columns = offset + lax.iota(jnp.int32, width)

    def add_term(position, total):
        ids_now = lax.dynamic_index_in_dim(query_terms, position, 1, keepdims=True)
        weight_now = (
            lax.dynamic_index_in_dim(query_levels, position, 1, keepdims=True).astype(jnp.float32)
            / 100.0
        )
        return total + jnp.where(ids_now == columns[None, :], weight_now, 0.0)

    initial = jnp.zeros((query_terms.shape[0], width), jnp.float32)
    return lax.fori_loop(0, query_terms.shape[1], add_term, initial)


def score_block(query_rows, postings):
    return lax.dot_general(
        query_rows, postings, (((1,), (1,)), ((), ())), preferred_element_type=jnp.float32
    )


def per_device(postings, query_terms, query_levels, feedback_ids):
    doc_rows, width = postings.shape
    queries = query_terms.shape[0]
    term_groups = lax.axis_size("term")
    group_rows = queries // term_groups
    term_index = lax.axis_index("term")
    doc_index = lax.axis_index("doc")
    query_part = query_slice(query_terms, query_levels, width, term_index * width)
    query_rounded = query_part.astype(jnp.bfloat16)
    local_slot = feedback_ids - doc_index * doc_rows
    positions = lax.iota(jnp.int32, doc_rows)
    selector = (local_slot[:, :, None] == positions[None, None, :]).astype(jnp.float32)
    partial_scores = score_block(query_rounded, postings)
    first_all = lax.psum(partial_scores, "term")
    first_scores = lax.dynamic_slice_in_dim(first_all, term_index * group_rows, group_rows, 0)
    feedback = jnp.sum(selector * first_all[:, None, :], axis=2).astype(jnp.bfloat16)
    feedback_wide = feedback.astype(jnp.float32)
    mixing = jnp.sum(selector * feedback_wide[:, :, None], axis=1).astype(jnp.bfloat16)
    numerator = jnp.dot(mixing, postings, preferred_element_type=jnp.float32)
    weight_part = jnp.sum(feedback_wide, axis=1)
    numerator_all, weight_sum = lax.psum((numerator, weight_part), "doc")
    expanded = (query_part + expansion_weight * numerator_all / weight_sum[:, None]).astype(
        jnp.bfloat16
    )
    final_scores = lax.psum_scatter(
        score_block(expanded, postings), "term", scatter_dimension=0, tiled=True
    )
    return (first_scores, final_scores)


def solution(mesh):
    return jax.shard_map(
        per_device,
        mesh=mesh,
        in_specs=(P("doc", "term"), P(), P(), P()),
        out_specs=(P("term", "doc"), P("term", "doc")),
        check_vma=False,
    )
```

profile of v0, /device:TPU:6, one launch (start us, length us, event | category | flops | bytes accessed | tf_op | source)
XLA Modules:
  0.0 416.9 jit_solution(17886859265091422871)
XLA Ops:
  7.2 53.6 %while.14 = (s32[]{:T(128)}, f32[128,1920]{1,0:T(8,128)S(1)}, s32[128,32]{0,1:T(8,128)}, s32[128,32]{0,1:T(8,128)}, s32[]{:T(128)}, /*index=5*/s32[]{:T(128)}, s32[]{:T(128)}) while((s32[]{:T(128)}, f32[128,1920]{1,0:T(8,128)S(1)}, s32[128,32]{0,1:T(8,128)}, s32[128,32]{0,1:T(8,128)}, s32[]{:T(128)}, /*index=5*/s32[]{:T(128)}, ...), condition=%wide.region_1.2_spmd.clone, body=%wide.region_0.1_spmd.clone.sunk | while | flops 985219 | bytes 1984619 | solution.py:21
  7.3 0.8 multiply_bitcast_fusion.2
  9.1 0.7 multiply_bitcast_fusion.2
  10.7 0.7 multiply_bitcast_fusion.2
  14.1 0.7 multiply_bitcast_fusion.2
  15.7 0.7 multiply_bitcast_fusion.2
  17.4 0.7 multiply_bitcast_fusion.2
  19.1 0.7 multiply_bitcast_fusion.2
  22.4 0.7 multiply_bitcast_fusion.2
  24.1 0.7 multiply_bitcast_fusion.2
  27.4 0.7 multiply_bitcast_fusion.2
  29.1 0.7 multiply_bitcast_fusion.2
  32.4 0.7 multiply_bitcast_fusion.2
  34.1 0.7 multiply_bitcast_fusion.2
  35.8 0.7 multiply_bitcast_fusion.2
  37.5 0.7 multiply_bitcast_fusion.2
  40.8 0.7 multiply_bitcast_fusion.2
  42.5 0.7 multiply_bitcast_fusion.2
  45.8 0.7 multiply_bitcast_fusion.2
  47.5 0.7 multiply_bitcast_fusion.2
  49.2 0.7 multiply_bitcast_fusion.2
  50.8 0.7 multiply_bitcast_fusion.2
  54.2 0.7 multiply_bitcast_fusion.2
  60.9 1.5 fusion.5
  62.4 140.0 %all-reduce.3.cloned.1.call-done = f32[128,512]{1,0:T(8,128)} async-done(((f32[128,512]{1,0:T(8,128)}), f32[128,512]{1,0:T(8,128)}) %all-reduce.3.cloned.1.call-update) | async-done | bytes 262160 | tf_op jit(solution)/shard_map/psum | solution.py:43
  202.4 1.5 select_reduce_fusion.1
  204.4 1.4 fusion.11
  205.9 53.0 %psum.23 = f32[128]{0:T(128)S(1)} all-reduce(f32[128]{0:T(128)S(1)} %fusion.9), channel_id=1, replica_groups=mesh['term'=16,'doc'=32] {'doc'}, use_global_device_ids=true, to_apply=%region_7.8 | all-reduce | flops 128 | bytes 1024 | tf_op jit(solution)/shard_map/psum | solution.py:50
  258.9 79.8 %all-reduce.5.cloned.1.call-done = f32[128,1920]{1,0:T(8,128)} async-done(((f32[128,1920]{1,0:T(8,128)}), f32[128,1920]{1,0:T(8,128)}) %all-reduce.5.cloned.1.call-update) | async-done | bytes 983056 | tf_op jit(solution)/shard_map/psum | solution.py:50
  338.7 2.7 fusion.2
  341.4 1.3 constant_dynamic-slice_fusion
  342.8 67.6 %reduce-scatter.2.cloned.1.call-done = f32[8,512]{1,0:T(8,128)} async-done(((f32[128,512]{1,0:T(8,128)}), f32[8,512]{1,0:T(8,128)}) %reduce-scatter.2.cloned.1.call-update) | async-done | bytes 16400 | tf_op jit(solution)/shard_map/reduce_scatter | solution.py:54
  (121 shorter events, 37.9 us)
Async XLA Ops:
  7.2 53.7 %copy-start = (bf16[512,1920]{1,0:T(8,128)(2,1)S(1)}, bf16[512,1920]{1,0:T(8,128)(2,1)}, u32[]{:S(2)}) copy-start(bf16[512,1920]{1,0:T(8,128)(2,1)} %param.6) | copy-start | bytes 5898244
  7.2 195.3 %all-reduce.3.cloned.1.call-start = ((), (), s32[]{:S(2)}) async-start(), calls=%async_computation.1 | async-start | bytes 524288 | tf_op jit(solution)/shard_map/psum | solution.py:43
  60.8 1.6 copy-start.1
  62.4 276.4 %all-reduce.5.cloned.1.call-start = ((), (), s32[]{:S(2)}) async-start(), calls=%async_computation.2 | async-start | bytes 1966080 | tf_op jit(solution)/shard_map/psum | solution.py:50
  205.8 204.5 %reduce-scatter.2.cloned.1.call-start = ((), (), s32[]{:S(2)}) async-start(), calls=%async_computation.3 | async-start | bytes 278528 | tf_op jit(solution)/shard_map/reduce_scatter | solution.py:54
Sparse Core Ops, SparseCore 0:
  62.5 139.9 all-reduce.2
  206.0 132.6 all-reduce.4
  342.1 68.2 reduce-scatter.1
where the time goes:
time: 420 us; the launch traced here: 417 us
  waiting for transfers between devices  287 us (68%)
  blocking collectives  53 us (13%)
  other arithmetic  32.6 us (8%)
  local copies, waits for them, and re-layouts  23.5 us (6%)
  between operations  13.8 us (3%)
  matrix products  5.59 us (1%)
    psum x1, waiting for transfers between devices, per_device(): first_all = lax.psum(partial_scores, 'term')  140 us
    psum x1, waiting for transfers between devices, per_device(): numerator_all, weight_sum = lax.psum((numerator, weight_part), 'doc')  79.8 us
    reduce_scatter x1, waiting for transfers between devices, per_device(): lax.psum_scatter(score_block(expanded, postings), 'term', scatter_dimensi...  67.6 us
    psum x1, blocking collectives, per_device(): numerator_all, weight_sum = lax.psum((numerator, weight_part), 'doc')  53 us
    broadcast_in_dim x32, other arithmetic, add_term(): return total + jnp.where(ids_now == columns[None, :], weight_now, 0.0)  22.5 us
    eq x32, local copies, waits for them, and re-layouts, add_term(): return total + jnp.where(ids_now == columns[None, :], weight_now, 0.0)  22.1 us
  transfers between devices with their start and end apart: 3, of which 3 were waited for; matrix products, arithmetic and copies ran while one was open for 0% of the time, Pallas kernels for 0%

commit v1 on v0

--- a/solution.py
+++ b/solution.py
@@ -40,7 +40,11 @@
     positions = lax.iota(jnp.int32, doc_rows)
     selector = (local_slot[:, :, None] == positions[None, None, :]).astype(jnp.float32)
     partial_scores = score_block(query_rounded, postings)
-    first_all = lax.psum(partial_scores, "term")
+    first_all = partial_scores
+    for hop in (1, 2, 4, 8):
+        first_all = first_all + lax.ppermute(
+            first_all, "term", [(dev, dev ^ hop) for dev in range(16)]
+        )
     first_scores = lax.dynamic_slice_in_dim(first_all, term_index * group_rows, group_rows, 0)
     feedback = jnp.sum(selector * first_all[:, None, :], axis=2).astype(jnp.bfloat16)
     feedback_wide = feedback.astype(jnp.float32)

time: 420 us -> 371 us (0.88)
  waiting for transfers between devices: 287 us -> 200 us
  starting transfers between devices: 0.12 us -> 37.1 us
    psum x1 -> x0, waiting for transfers between devices: 140 us -> none  [per_device(): first_all = lax.psum(partial_scores, 'term')]
    ppermute x0 -> x4, waiting for transfers between devices: none -> 53.6 us  [per_device(): lax.ppermute(first_all, 'term', [(dev, dev ^ hop) for dev in range(16)])]
    ppermute x0 -> x4, starting transfers between devices: none -> 37 us  [per_device(): lax.ppermute(first_all, 'term', [(dev, dev ^ hop) for dev in range(16)])]
  transfers between devices with their start and end apart: 3 -> 6, of which waited for: 3 -> 6; matrix products, arithmetic and copies ran while one was open for 0% -> 0% of each run, Pallas kernels for 0% -> 0%
where the time goes in v1:
time: 371 us; the launch traced here: 368 us
  waiting for transfers between devices  200 us (54%)
  blocking collectives  56 us (15%)
  starting transfers between devices  37.1 us (10%)
  other arithmetic  32.8 us (9%)
  local copies, waits for them, and re-layouts  22.7 us (6%)
  between operations  14.2 us (4%)
  matrix products  4.9 us (1%)
    psum x1, waiting for transfers between devices, per_device(): numerator_all, weight_sum = lax.psum((numerator, weight_part), 'doc')  77.8 us
    reduce_scatter x1, waiting for transfers between devices, per_device(): lax.psum_scatter(score_block(expanded, postings), 'term', scatter_dimensi...  68.5 us
    psum x1, blocking collectives, per_device(): numerator_all, weight_sum = lax.psum((numerator, weight_part), 'doc')  56 us
    ppermute x4, waiting for transfers between devices, per_device(): lax.ppermute(first_all, 'term', [(dev, dev ^ hop) for dev in range(16)])  53.6 us
    ppermute x4, starting transfers between devices, per_device(): lax.ppermute(first_all, 'term', [(dev, dev ^ hop) for dev in range(16)])  37 us
    broadcast_in_dim x32, other arithmetic, add_term(): return total + jnp.where(ids_now == columns[None, :], weight_now, 0.0)  22.5 us
    eq x32, local copies, waits for them, and re-layouts, add_term(): return total + jnp.where(ids_now == columns[None, :], weight_now, 0.0)  22.1 us
    add x32, other arithmetic, add_term(): return total + jnp.where(ids_now == columns[None, :], weight_now, 0.0)  8.05 us
  transfers between devices with their start and end apart: 6, of which 6 were waited for; matrix products, arithmetic and copies ran while one was open for 0% of the time, Pallas kernels for 0%

profile of v1, /device:TPU:6, one launch (start us, length us, event | category | flops | bytes accessed | tf_op | source)
XLA Modules:
  0.0 368.4 jit_solution(8282652637267309129)
XLA Ops:
  7.2 53.6 %while.14 = (s32[]{:T(128)}, f32[128,1920]{1,0:T(8,128)S(1)}, s32[128,32]{0,1:T(8,128)}, s32[128,32]{0,1:T(8,128)}, s32[]{:T(128)}, /*index=5*/s32[]{:T(128)}, s32[]{:T(128)}) while((s32[]{:T(128)}, f32[128,1920]{1,0:T(8,128)S(1)}, s32[128,32]{0,1:T(8,128)}, s32[128,32]{0,1:T(8,128)}, s32[]{:T(128)}, /*index=5*/s32[]{:T(128)}, ...), condition=%wide.region_1.2_spmd.clone, body=%wide.region_0.1_spmd.clone.sunk | while | flops 985219 | bytes 1984619 | solution.py:21
  7.3 0.8 multiply_bitcast_fusion.2
  9.1 0.7 multiply_bitcast_fusion.2
  10.7 0.7 multiply_bitcast_fusion.2
  14.1 0.7 multiply_bitcast_fusion.2
  15.7 0.7 multiply_bitcast_fusion.2
  17.4 0.7 multiply_bitcast_fusion.2
  19.1 0.7 multiply_bitcast_fusion.2
  22.4 0.7 multiply_bitcast_fusion.2
  24.1 0.7 multiply_bitcast_fusion.2
  27.4 0.7 multiply_bitcast_fusion.2
  29.1 0.7 multiply_bitcast_fusion.2
  32.4 0.7 multiply_bitcast_fusion.2
  34.1 0.7 multiply_bitcast_fusion.2
  35.8 0.7 multiply_bitcast_fusion.2
  37.5 0.7 multiply_bitcast_fusion.2
  40.8 0.7 multiply_bitcast_fusion.2
  60.9 0.8 fusion.5
  61.6 3.8 %collective-permute-start = (f32[128,512]{1,0:T(8,128)S(1)}, f32[128,512]{1,0:T(8,128)S(1)}, u32[]{:S(2)}, u32[]{:S(2)}) collective-permute-start(f32[128,512]{1,0:T(8,128)S(1)} %fusion.5), channel_id=1, source_target_pairs={{0,32},{32,0},{64,96},{96,64},{128,160},{160,128},{192,224},{224,1... | collective-permute-start | bytes 786440 | tf_op jit(solution)/shard_map/ppermute | solution.py:45
  65.5 6.3 %collective-permute-done = f32[128,512]{1,0:T(8,128)S(1)} collective-permute-done((f32[128,512]{1,0:T(8,128)S(1)}, f32[128,512]{1,0:T(8,128)S(1)}, u32[]{:S(2)}, u32[]{:S(2)}) %collective-permute-start) | collective-permute-done | bytes 262176 | tf_op jit(solution)/shard_map/ppermute | solution.py:45
  71.8 5.2 %collective-permute-start.1 = (f32[128,512]{1,0:T(8,128)S(1)}, f32[128,512]{1,0:T(8,128)S(1)}, u32[]{:S(2)}, u32[]{:S(2)}) collective-permute-start(f32[128,512]{1,0:T(8,128)S(1)} %add.62), channel_id=1, source_target_pairs={{0,64},{32,96},{64,0},{96,32},{128,192},{160,224},{192,128},{224,1... | collective-permute-start | bytes 786440 | tf_op jit(solution)/shard_map/ppermute | solution.py:45
  77.0 11.2 %collective-permute-done.1 = f32[128,512]{1,0:T(8,128)S(1)} collective-permute-done((f32[128,512]{1,0:T(8,128)S(1)}, f32[128,512]{1,0:T(8,128)S(1)}, u32[]{:S(2)}, u32[]{:S(2)}) %collective-permute-start.1) | collective-permute-done | bytes 262176 | tf_op jit(solution)/shard_map/ppermute | solution.py:45
  88.3 9.1 %collective-permute-start.2 = (f32[128,512]{1,0:T(8,128)S(1)}, f32[128,512]{1,0:T(8,128)S(1)}, u32[]{:S(2)}, u32[]{:S(2)}) collective-permute-start(f32[128,512]{1,0:T(8,128)S(1)} %add.63), channel_id=1, source_target_pairs={{0,128},{32,160},{64,192},{96,224},{128,0},{160,32},{192,64},{224,... | collective-permute-start | bytes 786440 | tf_op jit(solution)/shard_map/ppermute | solution.py:45
  97.4 21.3 %collective-permute-done.2 = f32[128,512]{1,0:T(8,128)S(1)} collective-permute-done((f32[128,512]{1,0:T(8,128)S(1)}, f32[128,512]{1,0:T(8,128)S(1)}, u32[]{:S(2)}, u32[]{:S(2)}) %collective-permute-start.2) | collective-permute-done | bytes 262176 | tf_op jit(solution)/shard_map/ppermute | solution.py:45
  118.7 18.9 %collective-permute-start.3 = (f32[128,512]{1,0:T(8,128)S(1)}, f32[128,512]{1,0:T(8,128)}, u32[]{:S(2)}, u32[]{:S(2)}) collective-permute-start(f32[128,512]{1,0:T(8,128)S(1)} %add.64), channel_id=1, source_target_pairs={{0,256},{32,288},{64,320},{96,352},{128,384},{160,416},{192,448},{... | collective-permute-start | bytes 786440 | tf_op jit(solution)/shard_map/ppermute | solution.py:45
  137.7 14.8 %collective-permute-done.3 = f32[128,512]{1,0:T(8,128)} collective-permute-done((f32[128,512]{1,0:T(8,128)S(1)}, f32[128,512]{1,0:T(8,128)}, u32[]{:S(2)}, u32[]{:S(2)}) %collective-permute-start.3) | collective-permute-done | bytes 262176 | tf_op jit(solution)/shard_map/ppermute | solution.py:45
  152.4 1.0 add.65
  154.4 1.4 fusion.11
  156.0 56.0 %psum.15 = f32[128]{0:T(128)S(1)} all-reduce(f32[128]{0:T(128)S(1)} %fusion.9), channel_id=1, replica_groups=mesh['term'=16,'doc'=32] {'doc'}, use_global_device_ids=true, to_apply=%region_6.7 | all-reduce | flops 128 | bytes 1024 | tf_op jit(solution)/shard_map/psum | solution.py:54
  212.0 77.8 %all-reduce.2.cloned.1.call-done = f32[128,1920]{1,0:T(8,128)} async-done(((f32[128,1920]{1,0:T(8,128)}), f32[128,1920]{1,0:T(8,128)}) %all-reduce.2.cloned.1.call-update) | async-done | bytes 983056 | tf_op jit(solution)/shard_map/psum | solution.py:54
  289.7 2.7 fusion.2
  293.1 68.5 %reduce-scatter.2.cloned.1.call-done = f32[8,512]{1,0:T(8,128)} async-done(((f32[128,512]{1,0:T(8,128)}), f32[8,512]{1,0:T(8,128)}) %reduce-scatter.2.cloned.1.call-update) | async-done | bytes 16400 | tf_op jit(solution)/shard_map/reduce_scatter | solution.py:58
  (130 shorter events, 43.3 us)
Async XLA Ops:
  7.2 53.7 %copy-start = (bf16[512,1920]{1,0:T(8,128)(2,1)S(1)}, bf16[512,1920]{1,0:T(8,128)(2,1)}, u32[]{:S(2)}) copy-start(bf16[512,1920]{1,0:T(8,128)(2,1)} %param.6) | copy-start | bytes 5898244
  7.2 282.5 %all-reduce.2.cloned.1.call-start = ((), (), s32[]{:S(2)}) async-start(), calls=%async_computation.1 | async-start | bytes 1966080 | tf_op jit(solution)/shard_map/psum | solution.py:54
  61.6 76.0 %copy-start.1 = (s32[128,10]{0,1:T(8,128)S(1)}, s32[128,10]{0,1:T(8,128)}, u32[]{:S(2)}) copy-start(s32[128,10]{0,1:T(8,128)} %param.9) | copy-start | bytes 15364
  61.6 10.1 %collective-permute-start = (f32[128,512]{1,0:T(8,128)S(1)}, f32[128,512]{1,0:T(8,128)S(1)}, u32[]{:S(2)}, u32[]{:S(2)}) collective-permute-start(f32[128,512]{1,0:T(8,128)S(1)} %fusion.5), channel_id=1, source_target_pairs={{0,32},{32,0},{64,96},{96,64},{128,160},{160,128},{192,224},{224,1... | collective-permute-start | bytes 786440 | tf_op jit(solution)/shard_map/ppermute | solution.py:45
  71.8 16.4 %collective-permute-start.1 = (f32[128,512]{1,0:T(8,128)S(1)}, f32[128,512]{1,0:T(8,128)S(1)}, u32[]{:S(2)}, u32[]{:S(2)}) collective-permute-start(f32[128,512]{1,0:T(8,128)S(1)} %add.62), channel_id=1, source_target_pairs={{0,64},{32,96},{64,0},{96,32},{128,192},{160,224},{192,128},{224,1... | collective-permute-start | bytes 786440 | tf_op jit(solution)/shard_map/ppermute | solution.py:45
  88.3 30.4 %collective-permute-start.2 = (f32[128,512]{1,0:T(8,128)S(1)}, f32[128,512]{1,0:T(8,128)S(1)}, u32[]{:S(2)}, u32[]{:S(2)}) collective-permute-start(f32[128,512]{1,0:T(8,128)S(1)} %add.63), channel_id=1, source_target_pairs={{0,128},{32,160},{64,192},{96,224},{128,0},{160,32},{192,64},{224,... | collective-permute-start | bytes 786440 | tf_op jit(solution)/shard_map/ppermute | solution.py:45
  118.7 33.7 %collective-permute-start.3 = (f32[128,512]{1,0:T(8,128)S(1)}, f32[128,512]{1,0:T(8,128)}, u32[]{:S(2)}, u32[]{:S(2)}) collective-permute-start(f32[128,512]{1,0:T(8,128)S(1)} %add.64), channel_id=1, source_target_pairs={{0,256},{32,288},{64,320},{96,352},{128,384},{160,416},{192,448},{... | collective-permute-start | bytes 786440 | tf_op jit(solution)/shard_map/ppermute | solution.py:45
  155.9 205.7 %reduce-scatter.2.cloned.1.call-start = ((), (), s32[]{:S(2)}) async-start(), calls=%async_computation.2 | async-start | bytes 278528 | tf_op jit(solution)/shard_map/reduce_scatter | solution.py:58
Sparse Core Ops, SparseCore 0:
  156.0 133.6 all-reduce.1
  293.3 68.2 reduce-scatter.1
